TPU v7x, 512 devices: a whole 4x8x8 slice. The times are simulated.
512 devices in a mesh: rep: 8 (over z_hi, core), fsdp: 64 (over y, x, z_lo).
Axes of the slice: x: 4, y: 8, z: 8 (z_hi: 4, z_lo: 2; z = z_hi * 2 + z_lo), core: 2. Of those that a mesh axis runs over, the one named last changes fastest.
Arguments:
- acts: bfloat16 [8, 8192, 8192], P('rep', 'fsdp'), may hold values from -16 to 16
- value_cots: bfloat16 [8, 8192, 512], P('rep', 'fsdp'), may hold values from -0.059814453 to 0.059814453
- inner_weights: float32 [8, 8192, 512], P('rep', 'fsdp'), may hold values from -0.0625 to 0.0625
- first_moment: float32 [8, 8192, 512], P('rep', 'fsdp'), may hold values from -1.8 to 1.8
- second_moment: float32 [8, 8192, 512], P('rep', 'fsdp'), may hold values from 0.01 to 1
- anchor: float32 [8192, 512], P('fsdp'), may hold values from -0.0625 to 0.0625
- outer_momentum: float32 [8192, 512], P('fsdp'), may hold values from -0.06 to 0.06
Outputs:
- first_next: float32 [8, 8192, 512], P('rep', 'fsdp')
- values_next: bfloat16 [8, 8192, 512], P('rep', 'fsdp')
All inputs are finite; a program needn't handle non-finite values.
Results may differ from a plain program's by a relative error of at most 0.0049.
Values may be sent and summed in bfloat16 or wider, within the bound.
A program may use at most 64 MiB of HBM per device.

v0:
```python
import jax
import jax.numpy as jnp
from jax import lax
from jax.sharding import PartitionSpec as P

decay_first = 0.9
decay_second = 0.95
inner_rate = 0.006
epsilon = 1e-08
outer_rate = 0.7
outer_decay = 0.9


def outer_update(average, anchor_rows, momentum_rows):
    velocity = outer_decay * momentum_rows + average
    return (anchor_rows - outer_rate * (average + outer_decay * velocity)).astype(jnp.bfloat16)


def on_device(acts, value_cots, inner_weights, first_moment, second_moment, anchor, outer_momentum):
    tokens_local = acts[0]
    cots_local = value_cots[0]
    rep_count = lax.axis_size("rep")
    feature_split = lax.all_to_all(tokens_local, "fsdp", split_axis=1, concat_axis=0, tiled=True)
    columns = feature_split
    gradient = lax.dot_general(
        columns,
        lax.all_gather(cots_local, "fsdp", axis=0, tiled=True),
        (((0,), (0,)), ((), ())),
        preferred_element_type=jnp.float32,
    )
    first_next = decay_first * first_moment[0] + (1.0 - decay_first) * gradient
    second_next = decay_second * second_moment[0] + (1.0 - decay_second) * gradient * gradient
    stepped = inner_weights[0] - inner_rate * first_next / (jnp.sqrt(second_next) + epsilon)
    drift = anchor - stepped
    summed_drift = lax.psum(drift, "rep")
    weights_next = outer_update(summed_drift / rep_count, anchor, outer_momentum)
    columns = tokens_local
    values = jnp.dot(
        columns,
        lax.all_gather(weights_next, "fsdp", axis=0, tiled=True),
        preferred_element_type=jnp.float32,
    )
    return (first_next[None], values.astype(jnp.bfloat16)[None])


def solution(mesh):
    placed = (
        P("rep", "fsdp", None),
        P("rep", "fsdp", None),
        P("rep", "fsdp", None),
        P("rep", "fsdp", None),
        P("rep", "fsdp", None),
        P("fsdp", None),
        P("fsdp", None),
    )
    return jax.shard_map(
        on_device,
        mesh=mesh,
        in_specs=placed,
        out_specs=(P("rep", "fsdp", None), P("rep", "fsdp", None)),
        check_vma=False,
    )
```

profile of v0, /device:TPU:2, one launch (start us, length us, event | category | flops | bytes accessed | tf_op | source)
XLA Modules:
  0.0 755.7 jit_solution(2856607011129081235)
XLA Ops:
  7.2 0.0 all-gather.6.cloned.1.call-start
  7.2 0.7 all-gather.6.cloned.1.call-update
  7.9 0.0 all-reduce.2.cloned.1.call-start
  7.9 3.2 copy.11
  11.2 74.7 %all_to_all.19 = bf16[128,64,128]{0,2,1:T(8,128)(2,1)} all-to-all(bf16[128,64,128]{0,2,1:T(8,128)(2,1)S(1)} %bitcast.35), channel_id=1, replica_groups=mesh['rep'=8,'fsdp'=64] {'fsdp'}, dimensions={1} | all-to-all | bytes 4194304 | tf_op jit(solution)/shard_map/all_to_all | solution.py:23
  85.9 0.0 copy-start
  85.9 0.0 copy-start.1
  85.9 3.3 copy.12
  89.2 248.0 %all-gather.6.cloned.1.call-done = bf16[1,8192,512]{2,1,0:T(8,128)(2,1)} async-done(((bf16[1,128,512]{2,1,0:T(8,128)(2,1)}), bf16[1,8192,512]{2,1,0:T(8,128)(2,1)}) %all-gather.6.cloned.1.call-update) | async-done | bytes 8388624 | tf_op jit(solution)/shard_map/all_gather | solution.py:27
  337.2 0.0 copy-done
  337.2 0.0 copy-done.1
  337.2 0.0 copy-done.2
  337.2 0.0 copy-done.3
  337.2 0.0 copy-start.4
  337.2 5.7 fusion.15
  342.9 0.0 all-reduce.2.cloned.1.call-update
  342.9 0.0 all-gather.4.cloned.1.call-start
  343.0 82.9 %all-reduce.2.cloned.1.call-done = f32[128,512]{1,0:T(8,128)} async-done(((f32[128,512]{1,0:T(8,128)}), f32[128,512]{1,0:T(8,128)}) %all-reduce.2.cloned.1.call-update) | async-done | bytes 262160 | tf_op jit(solution)/shard_map/psum | solution.py:35
  425.8 0.0 copy-done.4
  425.8 1.7 subtract_convert_fusion
  427.5 0.0 all-gather.4.cloned.1.call-update
  427.6 314.5 %all-gather.4.cloned.1.call-done = bf16[8192,512]{1,0:T(8,128)(2,1)} async-done(((bf16[128,512]{1,0:T(8,128)(2,1)}), bf16[8192,512]{1,0:T(8,128)(2,1)}) %all-gather.4.cloned.1.call-update) | async-done | bytes 8388624 | tf_op jit(solution)/shard_map/all_gather | solution.py:40
  742.1 6.4 fusion.7
  748.4 0.8 copy.13
  (2 shorter events, 0.0 us)
Async XLA Ops:
  7.2 330.1 %all-gather.6.cloned.1.call-start = ((), (), s32[]{:S(2)}) async-start(), calls=%async_computation.3 | async-start | bytes 8519680 | tf_op jit(solution)/shard_map/all_gather | solution.py:27
  7.9 417.9 %all-reduce.2.cloned.1.call-start = ((), (), s32[]{:S(2)}) async-start(), calls=%async_computation.1 | async-start | bytes 524288 | tf_op jit(solution)/shard_map/psum | solution.py:35
  85.9 251.4 %copy-start = (f32[128,512]{1,0:T(8,128)S(1)}, f32[128,512]{1,0:T(8,128)}, u32[]{:S(2)}) copy-start(f32[128,512]{1,0:T(8,128)} %param.12) | copy-start | bytes 786436
  85.9 251.4 %copy-start.1 = (f32[1,128,512]{2,1,0:T(8,128)S(1)}, f32[1,128,512]{2,1,0:T(8,128)}, u32[]{:S(2)}) copy-start(f32[1,128,512]{2,1,0:T(8,128)} %param.9) | copy-start | bytes 786436
  85.9 251.4 %copy-start.2 = (f32[1,128,512]{2,1,0:T(8,128)S(1)}, f32[1,128,512]{2,1,0:T(8,128)}, u32[]{:S(2)}) copy-start(f32[1,128,512]{2,1,0:T(8,128)} %param.11) | copy-start | bytes 786436
  85.9 251.4 %copy-start.3 = (f32[1,128,512]{2,1,0:T(8,128)S(1)}, f32[1,128,512]{2,1,0:T(8,128)}, u32[]{:S(2)}) copy-start(f32[1,128,512]{2,1,0:T(8,128)} %param.10) | copy-start | bytes 786436
  337.2 88.6 %copy-start.4 = (f32[128,512]{1,0:T(8,128)S(1)}, f32[128,512]{1,0:T(8,128)}, u32[]{:S(2)}) copy-start(f32[128,512]{1,0:T(8,128)} %param.13) | copy-start | bytes 786436
  342.9 399.1 %all-gather.4.cloned.1.call-start = ((), (), s32[]{:S(2)}) async-start(), calls=%async_computation.2 | async-start | bytes 8519680 | tf_op jit(solution)/shard_map/all_gather | solution.py:40
Sparse Core Ops, SparseCore 0:
  10.1 327.0 all-gather.5
  343.1 82.7 all-reduce.1
  428.7 313.3 all-gather.3
where the time goes:
time: 756 us
  waiting for transfers between devices  646 us (85%)
  blocking collectives  74.7 us (10%)
  between operations  13.8 us (2%)
  matrix products  12 us (2%)
    all_gather x1, waiting for transfers between devices, on_device(): lax.all_gather(weights_next, 'fsdp', axis=0, tiled=True)  315 us
    all_gather x1, waiting for transfers between devices, on_device(): lax.all_gather(cots_local, 'fsdp', axis=0, tiled=True)  248 us
    psum x1, waiting for transfers between devices, on_device(): summed_drift = lax.psum(drift, 'rep')  82.9 us
    all_to_all x1, blocking collectives, on_device(): lax.all_to_all(tokens_local, 'fsdp', split_axis=1, concat_axis=0, tiled=T...  74.7 us
  transfers between devices with their start and end apart: 3, of which 3 were waited for; matrix products, arithmetic and copies ran while one was open for 1% of the time, Pallas kernels for 0%

commit v1 on v0

--- a/solution.py
+++ b/solution.py
@@ -32,7 +32,7 @@
     second_next = decay_second * second_moment[0] + (1.0 - decay_second) * gradient * gradient
     stepped = inner_weights[0] - inner_rate * first_next / (jnp.sqrt(second_next) + epsilon)
     drift = anchor - stepped
-    summed_drift = lax.psum(drift, "rep")
+    summed_drift = jnp.sum(lax.all_gather(drift, "rep"), axis=0)
     weights_next = outer_update(summed_drift / rep_count, anchor, outer_momentum)
     columns = tokens_local
     values = jnp.dot(

time: 756 us -> 716 us (0.947)
  waiting for transfers between devices: 646 us -> 606 us
    psum x1 -> x0, waiting for transfers between devices: 82.9 us -> none  [on_device(): summed_drift = lax.psum(drift, 'rep')]
    all_gather x0 -> x1, waiting for transfers between devices: none -> 42.1 us  [on_device(): summed_drift = jnp.sum(lax.all_gather(drift, 'rep'), axis=0)]
where the time goes in v1:
time: 716 us
  waiting for transfers between devices  606 us (85%)
  blocking collectives  74.7 us (10%)
  between operations  13.8 us (2%)
  matrix products  11.4 us (2%)
  local copies, waits for them, and re-layouts  7.33 us (1%)
    all_gather x1, waiting for transfers between devices, on_device(): lax.all_gather(weights_next, 'fsdp', axis=0, tiled=True)  315 us
    all_gather x1, waiting for transfers between devices, on_device(): lax.all_gather(cots_local, 'fsdp', axis=0, tiled=True)  248 us
    all_to_all x1, blocking collectives, on_device(): lax.all_to_all(tokens_local, 'fsdp', split_axis=1, concat_axis=0, tiled=T...  74.7 us
    all_gather x1, waiting for transfers between devices, on_device(): summed_drift = jnp.sum(lax.all_gather(drift, 'rep'), axis=0)  42.1 us
  transfers between devices with their start and end apart: 3, of which 3 were waited for; matrix products, arithmetic and copies ran while one was open for 1% of the time, Pallas kernels for 0%

profile of v1, /device:TPU:2, one launch (start us, length us, event | category | flops | bytes accessed | tf_op | source)
XLA Modules:
  0.0 716.0 jit_solution(6697084526782444693)
XLA Ops:
  7.2 0.0 all-gather.8.cloned.1.call-start
  7.2 0.7 all-gather.8.cloned.1.call-update
  7.9 0.0 all-gather.10.cloned.1.call-start
  7.9 3.2 copy.11
  11.2 74.7 %all_to_all.19 = bf16[128,64,128]{0,2,1:T(8,128)(2,1)} all-to-all(bf16[128,64,128]{0,2,1:T(8,128)(2,1)S(1)} %bitcast.36), channel_id=1, replica_groups=mesh['rep'=8,'fsdp'=64] {'fsdp'}, dimensions={1} | all-to-all | bytes 4194304 | tf_op jit(solution)/shard_map/all_to_all | solution.py:23
  85.9 0.0 copy-start.1
  85.9 3.3 copy.12
  89.2 248.0 %all-gather.8.cloned.1.call-done = bf16[1,8192,512]{2,1,0:T(8,128)(2,1)} async-done(((bf16[1,128,512]{2,1,0:T(8,128)(2,1)}), bf16[1,8192,512]{2,1,0:T(8,128)(2,1)}) %all-gather.8.cloned.1.call-update) | async-done | bytes 8388624 | tf_op jit(solution)/shard_map/all_gather | solution.py:27
  337.2 0.0 copy-done.1
  337.2 0.0 copy-done.2
  337.2 0.0 copy-done.3
  337.2 0.0 copy-done.4
  337.2 5.6 fusion.15
  342.9 0.0 all-gather.10.cloned.1.call-update
  342.9 0.0 all-gather.6.cloned.1.call-start
  342.9 42.1 %all-gather.10.cloned.1.call-done = f32[1024,512]{1,0:T(8,128)} async-done(((f32[128,512]{1,0:T(8,128)}), f32[1024,512]{1,0:T(8,128)}) %all-gather.10.cloned.1.call-update) | async-done | bytes 2097168 | tf_op jit(solution)/shard_map/all_gather | solution.py:35
  385.0 1.8 reduce_sum.9
  386.9 0.0 copy-done.5
  386.9 0.7 subtract_convert_fusion
  387.6 0.0 all-gather.6.cloned.1.call-update
  387.6 315.3 %all-gather.6.cloned.1.call-done = bf16[8192,512]{1,0:T(8,128)(2,1)} async-done(((bf16[128,512]{1,0:T(8,128)(2,1)}), bf16[8192,512]{1,0:T(8,128)(2,1)}) %all-gather.6.cloned.1.call-update) | async-done | bytes 8388624 | tf_op jit(solution)/shard_map/all_gather | solution.py:40
  702.9 0.0 copy-done
  702.9 5.8 fusion.7
  708.7 0.8 copy.13
  (5 shorter events, 0.0 us)
Async XLA Ops:
  7.2 330.1 %all-gather.8.cloned.1.call-start = ((), (), s32[]{:S(2)}) async-start(), calls=%async_computation.2 | async-start | bytes 8519680 | tf_op jit(solution)/shard_map/all_gather | solution.py:27
  7.9 377.1 %all-gather.10.cloned.1.call-start = ((), (), s32[]{:S(2)}) async-start(), calls=%async_computation.3 | async-start | bytes 2359296 | tf_op jit(solution)/shard_map/all_gather | solution.py:35
  85.9 251.4 %copy-start.1 = (f32[128,512]{1,0:T(8,128)S(1)}, f32[128,512]{1,0:T(8,128)}, u32[]{:S(2)}) copy-start(f32[128,512]{1,0:T(8,128)} %param.12) | copy-start | bytes 786436
  85.9 251.4 %copy-start.2 = (f32[1,128,512]{2,1,0:T(8,128)S(1)}, f32[1,128,512]{2,1,0:T(8,128)}, u32[]{:S(2)}) copy-start(f32[1,128,512]{2,1,0:T(8,128)} %param.9) | copy-start | bytes 786436
  85.9 251.4 %copy-start.3 = (f32[1,128,512]{2,1,0:T(8,128)S(1)}, f32[1,128,512]{2,1,0:T(8,128)}, u32[]{:S(2)}) copy-start(f32[1,128,512]{2,1,0:T(8,128)} %param.11) | copy-start | bytes 786436
  85.9 251.4 %copy-start.4 = (f32[1,128,512]{2,1,0:T(8,128)S(1)}, f32[1,128,512]{2,1,0:T(8,128)}, u32[]{:S(2)}) copy-start(f32[1,128,512]{2,1,0:T(8,128)} %param.10) | copy-start | bytes 786436
  342.9 44.0 %copy-start.5 = (f32[128,512]{1,0:T(8,128)S(1)}, f32[128,512]{1,0:T(8,128)}, u32[]{:S(2)}) copy-start(f32[128,512]{1,0:T(8,128)} %param.13) | copy-start | bytes 786436
  342.9 360.1 %copy-start = (bf16[1,128,8192]{2,1,0:T(8,128)(2,1)S(1)}, bf16[1,128,8192]{2,1,0:T(8,128)(2,1)}, u32[]{:S(2)}) copy-start(bf16[1,128,8192]{2,1,0:T(8,128)(2,1)} %param.7) | copy-start | bytes 6291460
  342.9 360.0 %all-gather.6.cloned.1.call-start = ((), (), s32[]{:S(2)}) async-start(), calls=%async_computation.1 | async-start | bytes 8519680 | tf_op jit(solution)/shard_map/all_gather | solution.py:40
Sparse Core Ops, SparseCore 0:
  10.1 327.0 all-gather.7
  343.0 41.9 all-gather.9
  387.8 315.1 all-gather.5

commit v2 on v0

--- a/solution.py
+++ b/solution.py
@@ -37,7 +37,9 @@
     columns = tokens_local
     values = jnp.dot(
         columns,
-        lax.all_gather(weights_next, "fsdp", axis=0, tiled=True),
+        jnp.concatenate(
+            lax.all_to_all(jnp.stack([weights_next] * lax.axis_size("fsdp")), "fsdp", 0, 0), axis=0
+        ),
         preferred_element_type=jnp.float32,
     )
     return (first_next[None], values.astype(jnp.bfloat16)[None])

time: 756 us -> 633 us (0.84)
  the two profiles are of different devices: /device:TPU:2 before, /device:TPU:8 now
where the time goes in v2:
time: 633 us
  waiting for transfers between devices  329 us (52%)
  blocking collectives  272 us (43%)
  between operations  14.1 us (2%)
  local copies, waits for them, and re-layouts  8.34 us (1%)
  matrix products  8.06 us (1%)
    all_gather x1, waiting for transfers between devices, on_device(): lax.all_gather(cots_local, 'fsdp', axis=0, tiled=True)  239 us
    all_to_all x1, blocking collectives, on_device(): lax.all_to_all(jnp.stack([weights_next] * lax.axis_size('fsdp')), 'fsdp',...  195 us
    psum x1, waiting for transfers between devices, on_device(): summed_drift = lax.psum(drift, 'rep')  89.4 us
    all_to_all x1, blocking collectives, on_device(): lax.all_to_all(tokens_local, 'fsdp', split_axis=1, concat_axis=0, tiled=T...  77 us
  transfers between devices with their start and end apart: 2, of which 2 were waited for; matrix products, arithmetic and copies ran while one was open for 1% of the time, Pallas kernels for 0%

profile of v2, /device:TPU:8, one launch (start us, length us, event | category | flops | bytes accessed | tf_op | source)
XLA Modules:
  0.0 633.1 jit_solution(15325450039208415853)
XLA Ops:
  7.2 0.0 all-gather.3.cloned.1.call-start
  7.2 0.7 all-gather.3.cloned.1.call-update
  7.9 0.0 all-reduce.2.cloned.1.call-start
  7.9 3.2 copy.11
  11.2 77.0 %all_to_all.24 = bf16[128,64,128]{0,2,1:T(8,128)(2,1)} all-to-all(bf16[128,64,128]{0,2,1:T(8,128)(2,1)S(1)} %bitcast.37), channel_id=1, replica_groups=mesh['rep'=8,'fsdp'=64] {'fsdp'}, dimensions={1} | all-to-all | bytes 4194304 | tf_op jit(solution)/shard_map/all_to_all | solution.py:23
  88.2 0.0 copy-start.1
  88.2 3.3 copy.12
  91.5 239.2 %all-gather.3.cloned.1.call-done = bf16[1,8192,512]{2,1,0:T(8,128)(2,1)} async-done(((bf16[1,128,512]{2,1,0:T(8,128)(2,1)}), bf16[1,8192,512]{2,1,0:T(8,128)(2,1)}) %all-gather.3.cloned.1.call-update) | async-done | bytes 8388624 | tf_op jit(solution)/shard_map/all_gather | solution.py:27
  330.7 0.0 copy-done.1
  330.7 0.0 copy-done.2
  330.7 0.0 copy-done.3
  330.7 0.0 copy-done.4
  330.7 0.0 copy-start.5
  330.7 5.7 fusion.15
  336.4 0.0 all-reduce.2.cloned.1.call-update
  336.4 89.4 %all-reduce.2.cloned.1.call-done = f32[128,512]{1,0:T(8,128)} async-done(((f32[128,512]{1,0:T(8,128)}), f32[128,512]{1,0:T(8,128)}) %all-reduce.2.cloned.1.call-update) | async-done | bytes 262160 | tf_op jit(solution)/shard_map/psum | solution.py:35
  425.8 0.0 copy-done.5
  425.8 1.0 subtract_convert_fusion
  426.8 1.0 stack.2
  427.8 0.0 copy-start
  427.9 195.3 %all_to_all.25 = bf16[64,128,512]{2,1,0:T(8,128)(2,1)S(1)} all-to-all(bf16[64,128,512]{2,1,0:T(8,128)(2,1)S(1)} %stack.2), channel_id=1, replica_groups=mesh['rep'=8,'fsdp'=64] {'fsdp'}, dimensions={0} | all-to-all | bytes 16777216 | tf_op jit(solution)/shard_map/all_to_all | solution.py:41
  623.1 0.0 copy-done
  623.1 2.4 fusion.7
  625.5 0.8 copy.13
  (3 shorter events, 0.0 us)
Async XLA Ops:
  7.2 323.5 %all-gather.3.cloned.1.call-start = ((), (), s32[]{:S(2)}) async-start(), calls=%async_computation.3 | async-start | bytes 8519680 | tf_op jit(solution)/shard_map/all_gather | solution.py:27
  7.9 417.9 %all-reduce.2.cloned.1.call-start = ((), (), s32[]{:S(2)}) async-start(), calls=%async_computation.2 | async-start | bytes 524288 | tf_op jit(solution)/shard_map/psum | solution.py:35
  88.2 242.5 %copy-start.1 = (f32[128,512]{1,0:T(8,128)S(1)}, f32[128,512]{1,0:T(8,128)}, u32[]{:S(2)}) copy-start(f32[128,512]{1,0:T(8,128)} %param.12) | copy-start | bytes 786436
  88.2 242.5 %copy-start.2 = (f32[1,128,512]{2,1,0:T(8,128)S(1)}, f32[1,128,512]{2,1,0:T(8,128)}, u32[]{:S(2)}) copy-start(f32[1,128,512]{2,1,0:T(8,128)} %param.9) | copy-start | bytes 786436
  88.2 242.5 %copy-start.3 = (f32[1,128,512]{2,1,0:T(8,128)S(1)}, f32[1,128,512]{2,1,0:T(8,128)}, u32[]{:S(2)}) copy-start(f32[1,128,512]{2,1,0:T(8,128)} %param.11) | copy-start | bytes 786436
  88.2 242.5 %copy-start.4 = (f32[1,128,512]{2,1,0:T(8,128)S(1)}, f32[1,128,512]{2,1,0:T(8,128)}, u32[]{:S(2)}) copy-start(f32[1,128,512]{2,1,0:T(8,128)} %param.10) | copy-start | bytes 786436
  330.7 95.1 %copy-start.5 = (f32[128,512]{1,0:T(8,128)S(1)}, f32[128,512]{1,0:T(8,128)}, u32[]{:S(2)}) copy-start(f32[128,512]{1,0:T(8,128)} %param.13) | copy-start | bytes 786436
  427.8 195.3 %copy-start = (bf16[1,128,8192]{2,1,0:T(8,128)(2,1)S(1)}, bf16[1,128,8192]{2,1,0:T(8,128)(2,1)}, u32[]{:S(2)}) copy-start(bf16[1,128,8192]{2,1,0:T(8,128)(2,1)} %param.7) | copy-start | bytes 6291460
Sparse Core Ops, SparseCore 0:
  10.1 320.5 all-gather.2
  336.6 89.1 all-reduce.1
